TPU v7x, 128 devices: a whole 4x4x4 slice. The times are simulated.
128 devices in a mesh: hst: 4 (over z), dev: 32 (over y, x, core).
Axes of the slice: x: 4, y: 4, z: 4, core: 2. Of those that a mesh axis runs over, the one named last changes fastest.
Arguments:
- features: bfloat16 [262144, 768], P(('hst', 'dev')), may hold values from -6 to 6
- cache_blocks: bfloat16 [4, 8192, 768], P('hst', 'dev'), may hold values from -6 to 6
- plan: int32 [4, 64], P('hst', 'dev'), may hold values from 0 to 63, as said below
- miss_ids: int32 [128, 4, 32, 16], P(('hst', 'dev')), may hold values from 0 to 2303, as said below
- miss_counts: int32 [128, 4, 32], P(('hst', 'dev')), may hold values from 4 to 16, as said below
- self_ids: int32 [106496], P(('hst', 'dev')), may hold values from 0 to 2047, as said below
- nbr_ids: int32 [106496, 15], P(('hst', 'dev')), may hold values from 0 to 2047, as said below
- hop_counts: int32 [106496], P(('hst', 'dev')), may hold values from 1 to 15, as said below
- seed_counts: int32 [4096], P(('hst', 'dev')), may hold values from 1 to 25, as said below
- w_self1: bfloat16 [768, 1024], replicated, may hold values from -0.21875 to 0.21875
- w_nbr1: bfloat16 [768, 1024], replicated, may hold values from -0.21875 to 0.21875
- w_self2: bfloat16 [1024, 1024], replicated, may hold values from -0.1875 to 0.1875
- w_nbr2: bfloat16 [1024, 1024], replicated, may hold values from -0.1875 to 0.1875
- cotangent: bfloat16 [4096, 1024], P(('hst', 'dev')), may hold values from -1.25 to 1.25
Outputs:
- embedding: bfloat16 [4096, 1024], P(('hst', 'dev'))
- new_cache: bfloat16 [4, 8192, 768], P('hst', 'dev')
- grad_self1: float32 [768, 1024], P(None, ('hst', 'dev'))
- grad_nbr1: float32 [768, 1024], P(None, ('hst', 'dev'))
- grad_self2: float32 [1024, 1024], P(None, ('hst', 'dev'))
- grad_nbr2: float32 [1024, 1024], P(None, ('hst', 'dev'))
Inputs may be any that keep to these rules, and one draw needn't show every extreme that they name: Within each cache domain h, plan[h] is a permutation of the 64 block numbers. `miss_ids`: row numbers into the peer's served table; slots at or past the count are unused. `miss_counts`: in every draw some peer is asked for 16 rows by every device. `self_ids`: each names a used fetched slot p * 16 + c of the same device, c below that device's count for peer p. `nbr_ids`: each names a used fetched slot p * 16 + c of the same device, c below that device's count for peer p. `hop_counts`: the first node of every device has 15. `seed_counts`: the first seed of every device has 25.
All inputs are finite; a program needn't handle non-finite values.
Results may differ from a plain program's by a relative error of at most 0.0052.
Values may be sent and summed in bfloat16 or wider, within the bound.
No kernel may reach another device: no remote copies, remote signals or barrier semaphores. Data moves between devices by JAX's collectives and lax.ppermute only.
A program may use at most 128 MiB of HBM per device.

v0:
```python
import jax
import jax.numpy as jnp
from jax import lax
from jax.sharding import PartitionSpec as P

FAN1 = 25
FAN2 = 15
CSLOT = 2
BLOCK = 128


def local_step(
    frontier, self_rows, nbr_rows, count_one, count_two, w_self1, w_nbr1, w_self2, w_nbr2, cot_rows
):
    seed_count = count_two.shape[0]
    width = w_self2.shape[0]
    width_in = frontier.shape[1]
    own_rows = frontier[self_rows]
    mask_one = jnp.arange(FAN2, dtype=jnp.int32)[None, :] < count_one[:, None]
    summed_one = jnp.zeros((own_rows.shape[0], width_in), jnp.float32)
    for k in range(FAN2):
        picked = frontier[nbr_rows[:, k]].astype(jnp.float32)
        summed_one = summed_one + jnp.where(mask_one[:, k][:, None], picked, jnp.zeros_like(picked))
    mean_one = (summed_one / count_one[:, None].astype(jnp.float32)).astype(jnp.bfloat16)
    hidden_pre = jnp.dot(own_rows, w_self1, preferred_element_type=jnp.float32) + jnp.dot(
        mean_one, w_nbr1, preferred_element_type=jnp.float32
    )
    hidden_one = jax.nn.silu(hidden_pre).astype(jnp.bfloat16)
    seed_rows = hidden_one[:seed_count]
    hop_rows = hidden_one[seed_count:].reshape(seed_count, FAN1, width)
    mask_two = jnp.arange(FAN1, dtype=jnp.int32)[None, :] < count_two[:, None]
    summed_two = jnp.einsum(
        "skh,sk->sh", hop_rows, mask_two.astype(jnp.bfloat16), preferred_element_type=jnp.float32
    )
    mean_two = (summed_two / count_two[:, None].astype(jnp.float32)).astype(jnp.bfloat16)
    embedding = (
        jnp.dot(seed_rows, w_self2, preferred_element_type=jnp.float32)
        + jnp.dot(mean_two, w_nbr2, preferred_element_type=jnp.float32)
    ).astype(jnp.bfloat16)
    grad_self2 = jnp.dot(cot_rows.T, seed_rows, preferred_element_type=jnp.float32)
    grad_nbr2 = jnp.dot(cot_rows.T, mean_two, preferred_element_type=jnp.float32)
    back_self = jnp.dot(cot_rows, w_self2.T, preferred_element_type=jnp.float32)
    back_mean = jnp.dot(cot_rows, w_nbr2.T, preferred_element_type=jnp.float32) / count_two[
        :, None
    ].astype(jnp.float32)
    back_hop = back_mean[:, None, :] * mask_two.astype(jnp.float32)[:, :, None]
    back_hidden = jnp.concatenate([back_self, back_hop.reshape(seed_count * FAN1, width)], 0)
    gate_value = jax.nn.sigmoid(hidden_pre)
    back_pre = (back_hidden * gate_value * (1.0 + hidden_pre * (1.0 - gate_value))).astype(
        jnp.bfloat16
    )
    grad_self1 = jnp.dot(back_pre.T, own_rows, preferred_element_type=jnp.float32)
    grad_nbr1 = jnp.dot(back_pre.T, mean_one, preferred_element_type=jnp.float32)
    return (embedding, (grad_self1, grad_nbr1, grad_self2, grad_nbr2))


def local(
    features,
    cache_blocks,
    plan,
    miss_ids,
    miss_counts,
    self_ids,
    nbr_ids,
    hop_counts,
    seed_counts,
    w_self1,
    w_nbr1,
    w_self2,
    w_nbr2,
    cotangent,
):
    width_in = features.shape[1]
    slot_count = miss_ids.shape[3]
    device_count = lax.axis_size(("hst", "dev"))
    start_cache = jnp.zeros((CSLOT, BLOCK, width_in), jnp.bfloat16)
    current = start_cache
    shard_rows = lax.all_gather(cache_blocks, "dev", axis=1, tiled=True)
    block_count = shard_rows.shape[1] // BLOCK
    arrived = shard_rows[0].reshape(block_count, BLOCK, width_in)
    for target in range(CSLOT):
        offset = plan[0, target]
        inside = (offset >= 0) & (offset < block_count)
        chosen = lax.dynamic_index_in_dim(
            arrived, jnp.clip(offset, 0, block_count - 1), 0, keepdims=False
        )
        current = current.at[target].set(jnp.where(inside, chosen, current[target]))
    new_cache = current.reshape(1, CSLOT * BLOCK, width_in)
    lookup_table = jnp.concatenate([features, new_cache[0]], 0)
    requests = miss_ids.reshape(device_count, slot_count)
    row_data = lookup_table[
        lax.all_to_all(requests, ("hst", "dev"), split_axis=0, concat_axis=0, tiled=True)
    ]
    fetched = lax.all_to_all(row_data, ("hst", "dev"), split_axis=0, concat_axis=0, tiled=True)
    counted = miss_counts.reshape(device_count)
    is_valid = jnp.arange(slot_count, dtype=jnp.int32)[None, :] < counted[:, None]
    fetched = jnp.where(is_valid[:, :, None], fetched, jnp.zeros_like(fetched))
    frontier = fetched.reshape(device_count * slot_count, width_in)
    embedding, grads = local_step(
        frontier,
        self_ids,
        nbr_ids,
        hop_counts,
        seed_counts,
        w_self1,
        w_nbr1,
        w_self2,
        w_nbr2,
        cotangent,
    )
    share_self1, share_nbr1, share_self2, share_nbr2 = (
        lax.psum_scatter(grads[0], ("hst", "dev"), scatter_dimension=0, tiled=True),
        lax.psum_scatter(grads[1], ("hst", "dev"), scatter_dimension=0, tiled=True),
        lax.psum_scatter(grads[2], ("hst", "dev"), scatter_dimension=0, tiled=True),
        lax.psum_scatter(grads[3], ("hst", "dev"), scatter_dimension=0, tiled=True),
    )
    return (embedding, new_cache, share_self1.T, share_nbr1.T, share_self2.T, share_nbr2.T)


def solution(mesh):
    return jax.shard_map(
        local,
        mesh=mesh,
        in_specs=(
            P(("hst", "dev"), None),
            P("hst", "dev", None),
            P("hst", "dev"),
            P(("hst", "dev"), None, None, None),
            P(("hst", "dev"), None, None),
            P(("hst", "dev")),
            P(("hst", "dev"), None),
            P(("hst", "dev")),
            P(("hst", "dev")),
            P(),
            P(),
            P(),
            P(),
            P(("hst", "dev"), None),
        ),
        out_specs=(
            P(("hst", "dev"), None),
            P("hst", "dev", None),
            P(None, ("hst", "dev")),
            P(None, ("hst", "dev")),
            P(None, ("hst", "dev")),
            P(None, ("hst", "dev")),
        ),
        check_vma=False,
    )
```

profile of v0, /device:TPU:0, one launch (start us, length us, event | category | flops | bytes accessed | tf_op | source)
XLA Modules:
  0.0 2006.0 jit_solution(17963824004215073880)
XLA Ops:
  7.2 0.7 all-gather.2.cloned.1.call-update
  7.9 1.5 copy.32
  9.4 11.2 all-to-all-start
  20.6 1.3 fusion.28
  25.8 0.8 lt.138
  26.5 0.7 convert_element_type.95
  27.2 0.7 convert_element_type.98
  27.9 1.9 all-to-all-done
  29.9 45.5 %all-gather.2.cloned.1.call-done = bf16[1,8192,768]{2,1,0:T(8,128)(2,1)} async-done(((bf16[1,256,768]{2,1,0:T(8,128)(2,1)}), bf16[1,8192,768]{2,1,0:T(8,128)(2,1)}) %all-gather.2.cloned.1.call-update) | async-done | bytes 12582928 | tf_op jit(solution)/shard_map/all_gather | solution.py:78
  75.5 1.1 dynamic-slice_select_fusion.1
  76.6 0.7 copy-done.10
  77.3 3.9 pad_maximum_fusion
  81.3 12.6 gather_fusion
  93.8 8.7 all-to-all-start.1
  102.6 2.3 convolution_divide_fusion
  104.9 2.6 mul.30
  107.5 4.1 mul.31
  111.7 0.1 reshape.188
  111.8 0.2 fusion.11
  112.2 0.7 slice_reduce_fusion.14
  113.0 1.4 fusion.30
  114.4 3.9 broadcast_multiply_fusion
  118.3 25.5 %all-to-all-done.1 = bf16[128,16,768]{2,1,0:T(8,128)(2,1)} async-done(((bf16[128,16,768]{2,1,0:T(8,128)(2,1)}), bf16[128,16,768]{2,1,0:T(8,128)(2,1)}, u32[]{:S(2)}, u32[]{:S(2)}) %all-to-all-start.1) | async-done | bytes 3145760 | tf_op jit(solution)/shard_map/all_to_all | solution.py:94
  143.8 3.3 broadcast_select_fusion
  147.1 6.7 gather_fusion.10
  153.8 7.1 gather_fusion.11
  160.9 7.1 gather_fusion.12
  168.0 7.1 gather_fusion.13
  175.1 7.1 gather_fusion.14
  182.2 7.1 gather_fusion.15
  189.2 7.1 gather_fusion.16
  196.3 7.3 gather_fusion.3
  203.6 7.1 gather_fusion.4
  210.6 7.1 gather_fusion.5
  217.7 7.1 gather_fusion.6
  224.8 7.1 gather_fusion.7
  231.9 7.1 gather_fusion.8
  239.0 7.1 gather_fusion.9
  246.0 7.1 gather_fusion.2
  253.1 7.3 gather_fusion.1
  260.5 3.4 fusion.29
  264.0 0.1 copy-done.6
  264.1 0.4 copy-done.7
  264.5 0.4 copy-done.8
  264.9 8.8 divide_convert_fusion
  273.8 3.9 fusion.1
  277.6 1.2 copy-done.25
  278.8 3.5 fusion.32
  282.4 1.2 copy-done.11
  283.6 5.1 fusion.31
  288.8 2.7 slice.226
  291.5 2.7 reshape.186
  294.2 2.0 fusion.4
  296.2 2.8 convolution_bitcast_fusion
  299.0 5.4 copy.35
  304.5 3.6 convolution_bitcast_fusion.1
  308.1 5.4 copy.33
  313.5 1.5 fusion.7
  315.0 0.2 copy-done.1
  315.1 1.1 fusion.2
  316.3 172.0 %reduce-scatter.11.cloned.1.call-done = f32[8,768]{1,0:T(8,128)} async-done(((f32[1024,768]{1,0:T(8,128)}), f32[8,768]{1,0:T(8,128)}) %reduce-scatter.11.cloned.1.call-update) | async-done | bytes 24592 | tf_op jit(solution)/shard_map/reduce_scatter | solution.py:113
  488.3 213.3 %reduce-scatter.9.cloned.1.call-done = f32[8,768]{1,0:T(8,128)} async-done(((f32[1024,768]{1,0:T(8,128)}), f32[8,768]{1,0:T(8,128)}) %reduce-scatter.9.cloned.1.call-update) | async-done | bytes 24592 | tf_op jit(solution)/shard_map/reduce_scatter | solution.py:112
  701.6 650.9 %reduce-scatter.15.cloned.1.call-done = f32[8,1024]{1,0:T(8,128)} async-done(((f32[1024,1024]{1,0:T(8,128)}), f32[8,1024]{1,0:T(8,128)}) %reduce-scatter.15.cloned.1.call-update) | async-done | bytes 32784
  1352.5 646.7 %reduce-scatter.13.cloned.1.call-done = f32[8,1024]{1,0:T(8,128)} async-done(((f32[1024,1024]{1,0:T(8,128)}), f32[8,1024]{1,0:T(8,128)}) %reduce-scatter.13.cloned.1.call-update) | async-done | bytes 32784
  (71 shorter events, 0.7 us)
Async XLA Ops:
  7.2 105.8 %copy-start = (bf16[1024,1024]{1,0:T(8,128)(2,1)S(1)}, bf16[1024,1024]{1,0:T(8,128)(2,1)}, u32[]{:S(2)}) copy-start(bf16[1024,1024]{1,0:T(8,128)(2,1)} %param.29) | copy-start | bytes 6291460
  7.2 68.3 %all-gather.2.cloned.1.call-start = ((), (), s32[]{:S(2)}) async-start(), calls=%async_computation.6 | async-start | bytes 12976128 | tf_op jit(solution)/shard_map/all_gather | solution.py:78
  9.4 20.4 %all-to-all-start = ((s32[128,1,16]{2,1,0:T(1,128)}), s32[128,1,16]{2,1,0:T(1,128)S(1)}, u32[]{:S(2)}, u32[]{:S(2)}) async-start(s32[128,1,16]{2,1,0:T(1,128)} %bitcast.6), calls=%async_computation | async-start | bytes 131072 | tf_op jit(solution)/shard_map/all_to_all | solution.py:92
  76.6 0.7 copy-start.10
  93.8 8.8 copy-start.12
  93.8 50.0 %all-to-all-start.1 = ((bf16[128,16,768]{2,1,0:T(8,128)(2,1)}), bf16[128,16,768]{2,1,0:T(8,128)(2,1)}, u32[]{:S(2)}, u32[]{:S(2)}) async-start(bf16[128,16,768]{2,1,0:T(8,128)(2,1)} %bitcast.66), calls=%async_computation.1 | async-start | bytes 6291456 | tf_op jit(solution)/shard_map/all_to_all | solution.py:94
  102.6 385.7 %reduce-scatter.11.cloned.1.call-start = ((), (), s32[]{:S(2)}) async-start(), calls=%async_computation.8 | async-start | bytes 3170304 | tf_op jit(solution)/shard_map/reduce_scatter | solution.py:113
  107.5 4.1 copy-start.23
  107.5 4.3 copy-start.14
  107.5 4.5 copy-start.22
  107.5 4.6 copy-start.15
  260.4 3.5 copy-start.2
  260.4 3.6 copy-start.3
  260.4 3.6 copy-start.4
  260.4 3.6 copy-start.5
  260.4 3.7 copy-start.6
  260.4 4.1 copy-start.7
  260.5 4.4 copy-start.8
  260.5 4.4 copy-start.16
  260.5 4.4 copy-start.17
  260.5 4.4 copy-start.18
  260.5 4.4 copy-start.19
  260.5 4.4 copy-start.20
  260.5 4.4 copy-start.21
  264.9 8.8 copy-start.9
  264.9 8.8 copy-start.13
  264.9 8.8 copy-start.24
  277.6 1.2 copy-start.25
  282.3 1.3 copy-start.11
  282.4 419.2 %reduce-scatter.9.cloned.1.call-start = ((), (), s32[]{:S(2)}) async-start(), calls=%async_computation.7 | async-start | bytes 3170304 | tf_op jit(solution)/shard_map/reduce_scatter | solution.py:112
  288.7 1063.8 %reduce-scatter.15.cloned.1.call-start = ((), (), s32[]{:S(2)}) async-start(), calls=%async_computation.10 | async-start | bytes 4227072
  304.4 1694.8 %reduce-scatter.13.cloned.1.call-start = ((), (), s32[]{:S(2)}) async-start(), calls=%async_computation.9 | async-start | bytes 4227072
  313.5 1.6 copy-start.1
Sparse Core Ops, SparseCore 0:
  10.2 65.1 all-gather.1
  282.5 205.7 reduce-scatter.10
  493.7 207.9 reduce-scatter.8
  704.4 648.0 reduce-scatter.14
  1355.3 643.8 reduce-scatter.12
where the time goes:
time: 2010 us
  waiting for transfers between devices  1760 us (88%)
  local copies, waits for them, and re-layouts  158 us (8%)
  matrix products  30.5 us (2%)
  other arithmetic  22.8 us (1%)
  starting transfers between devices  20.1 us (1%)
    unnamed x7, waiting for transfers between devices  1300 us
    reduce_scatter x1, waiting for transfers between devices, local(): lax.psum_scatter(grads[0], ('hst', 'dev'), scatter_dimension=0, tiled=True)  213 us
    reduce_scatter x1, waiting for transfers between devices, local(): lax.psum_scatter(grads[1], ('hst', 'dev'), scatter_dimension=0, tiled=True)  172 us
    gather x15, local copies, waits for them, and re-layouts, local_step(): picked = frontier[nbr_rows[:, k]].astype(jnp.float32)  106 us
    all_gather x1, waiting for transfers between devices, local(): shard_rows = lax.all_gather(cache_blocks, 'dev', axis=1, tiled=True)  45.5 us
  transfers between devices with their start and end apart: 7, of which 7 were waited for; matrix products, arithmetic and copies ran while one was open for 3% of the time, Pallas kernels for 0%

commit v1 on v0

--- a/solution.py
+++ b/solution.py
@@ -75,7 +75,9 @@
     device_count = lax.axis_size(("hst", "dev"))
     start_cache = jnp.zeros((CSLOT, BLOCK, width_in), jnp.bfloat16)
     current = start_cache
-    shard_rows = lax.all_gather(cache_blocks, "dev", axis=1, tiled=True)
+    shard_rows = jnp.concatenate(
+        lax.all_to_all(jnp.stack([cache_blocks] * lax.axis_size("dev")), "dev", 0, 0), axis=1
+    )
     block_count = shard_rows.shape[1] // BLOCK
     arrived = shard_rows[0].reshape(block_count, BLOCK, width_in)
     for target in range(CSLOT):

time: 2010 us -> 2140 us (1.065)
  waiting for transfers between devices: 1760 us -> 1860 us
    all_to_all x1, waiting for transfers between devices: 1.92 us -> 156 us  [local(): lax.all_to_all(jnp.stack([cache_blocks] * lax.axis_size('dev')), 'dev', 0...]
    all_gather x1 -> x0, waiting for transfers between devices: 45.5 us -> none  [local(): shard_rows = lax.all_gather(cache_blocks, 'dev', axis=1, tiled=True)]
    unnamed x7 -> x6, waiting for transfers between devices: 1300 us -> 1300 us
  transfers between devices with their start and end apart: 7 -> 6, of which waited for: 7 -> 6; matrix products, arithmetic and copies ran while one was open for 3% -> 2% of each run, Pallas kernels for 0% -> 0%
where the time goes in v1:
time: 2140 us; the launch traced here: 2130 us
  waiting for transfers between devices  1860 us (87%)
  local copies, waits for them, and re-layouts  163 us (8%)
  matrix products  30.5 us (1%)
    unnamed x6, waiting for transfers between devices  1300 us
    reduce_scatter x1, waiting for transfers between devices, local(): lax.psum_scatter(grads[0], ('hst', 'dev'), scatter_dimension=0, tiled=True)  213 us
    reduce_scatter x1, waiting for transfers between devices, local(): lax.psum_scatter(grads[1], ('hst', 'dev'), scatter_dimension=0, tiled=True)  172 us
    all_to_all x1, waiting for transfers between devices, local(): lax.all_to_all(jnp.stack([cache_blocks] * lax.axis_size('dev')), 'dev', 0...  156 us
    gather x15, local copies, waits for them, and re-layouts, local_step(): picked = frontier[nbr_rows[:, k]].astype(jnp.float32)  106 us
  transfers between devices with their start and end apart: 6, of which 6 were waited for; matrix products, arithmetic and copies ran while one was open for 2% of the time, Pallas kernels for 0%

profile of v1, /device:TPU:0, one launch (start us, length us, event | category | flops | bytes accessed | tf_op | source)
XLA Modules:
  0.0 2129.3 jit_solution(14187907152749012379)
XLA Ops:
  7.2 1.0 copy.32
  8.2 20.3 all_to_all.22
  28.5 6.9 stack.2
  35.4 5.2 all-to-all-start
  40.6 0.6 fusion.28
  45.1 0.1 lt.138
  45.2 0.1 reshape.194
  45.3 155.7 %all-to-all-done = bf16[32,1,256,768]{3,2,1,0:T(8,128)(2,1)} async-done(((bf16[32,1,256,768]{3,2,1,0:T(8,128)(2,1)}), bf16[32,1,256,768]{3,2,1,0:T(8,128)(2,1)}, u32[]{:S(2)}, u32[]{:S(2)}) %all-to-all-start) | async-done | bytes 12582944 | tf_op jit(solution)/shard_map/all_to_all | solution.py:79
  201.0 1.1 dynamic-slice_select_fusion.1
  202.1 0.7 copy-done.10
  202.8 3.9 pad_maximum_fusion
  206.8 12.6 gather_fusion
  219.3 5.9 all-to-all-start.2
  225.3 2.3 convolution_divide_fusion
  227.6 2.6 mul.30
  230.2 4.1 mul.31
  234.3 0.1 reshape.191
  234.4 0.2 fusion.11
  234.8 0.7 slice_reduce_fusion.14
  235.5 0.1 iota_compare_fusion
  235.6 1.4 fusion.30
  237.0 3.9 broadcast_multiply_fusion
  240.9 25.6 %all-to-all-done.2 = bf16[128,16,768]{2,1,0:T(8,128)(2,1)} async-done(((bf16[128,16,768]{2,1,0:T(8,128)(2,1)}), bf16[128,16,768]{2,1,0:T(8,128)(2,1)}, u32[]{:S(2)}, u32[]{:S(2)}) %all-to-all-start.2) | async-done | bytes 3145760 | tf_op jit(solution)/shard_map/all_to_all | solution.py:96
  266.4 3.3 broadcast_select_fusion
  269.7 6.7 gather_fusion.10
  276.5 7.1 gather_fusion.11
  283.6 7.1 gather_fusion.12
  290.6 7.1 gather_fusion.13
  297.7 7.1 gather_fusion.14
  304.8 7.1 gather_fusion.15
  311.9 7.1 gather_fusion.16
  319.0 7.3 gather_fusion.3
  326.2 7.1 gather_fusion.4
  333.3 7.1 gather_fusion.5
  340.4 7.1 gather_fusion.6
  347.4 7.1 gather_fusion.7
  354.5 7.1 gather_fusion.8
  361.6 7.1 gather_fusion.9
  368.7 7.1 gather_fusion.2
  375.8 7.3 gather_fusion.1
  383.2 3.4 fusion.29
  386.7 0.1 copy-done.6
  386.8 0.4 copy-done.7
  387.1 0.4 copy-done.8
  387.6 8.8 divide_convert_fusion
  396.4 3.9 fusion.1
  400.3 1.2 copy-done.27
  401.4 3.5 fusion.32
  405.1 1.2 copy-done.11
  406.3 5.1 fusion.31
  411.4 2.7 slice.226
  414.1 2.7 reshape.189
  416.9 2.0 fusion.4
  418.9 2.8 convolution_bitcast_fusion
  421.7 5.4 copy.35
  427.2 3.6 convolution_bitcast_fusion.1
  430.7 5.4 copy.33
  436.1 1.5 fusion.7
  437.6 0.2 copy-done.1
  437.8 1.1 fusion.2
  438.9 172.1 %reduce-scatter.11.cloned.1.call-done = f32[8,768]{1,0:T(8,128)} async-done(((f32[1024,768]{1,0:T(8,128)}), f32[8,768]{1,0:T(8,128)}) %reduce-scatter.11.cloned.1.call-update) | async-done | bytes 24592 | tf_op jit(solution)/shard_map/reduce_scatter | solution.py:115
  611.0 213.4 %reduce-scatter.9.cloned.1.call-done = f32[8,768]{1,0:T(8,128)} async-done(((f32[1024,768]{1,0:T(8,128)}), f32[8,768]{1,0:T(8,128)}) %reduce-scatter.9.cloned.1.call-update) | async-done | bytes 24592 | tf_op jit(solution)/shard_map/reduce_scatter | solution.py:114
  824.4 651.3 %reduce-scatter.15.cloned.1.call-done = f32[8,1024]{1,0:T(8,128)} async-done(((f32[1024,1024]{1,0:T(8,128)}), f32[8,1024]{1,0:T(8,128)}) %reduce-scatter.15.cloned.1.call-update) | async-done | bytes 32784
  1475.6 646.9 %reduce-scatter.13.cloned.1.call-done = f32[8,1024]{1,0:T(8,128)} async-done(((f32[1024,1024]{1,0:T(8,128)}), f32[8,1024]{1,0:T(8,128)}) %reduce-scatter.13.cloned.1.call-update) | async-done | bytes 32784
  (74 shorter events, 0.6 us)
Async XLA Ops:
  7.2 228.4 %copy-start = (bf16[1024,1024]{1,0:T(8,128)(2,1)S(1)}, bf16[1024,1024]{1,0:T(8,128)(2,1)}, u32[]{:S(2)}) copy-start(bf16[1024,1024]{1,0:T(8,128)(2,1)} %param.29) | copy-start | bytes 6291460
  35.4 5.2 copy-start.24
  35.4 9.7 copy-start.23
  35.4 9.8 copy-start.15
  35.4 9.8 copy-start.25
  35.4 165.6 %all-to-all-start = ((bf16[32,1,256,768]{3,2,1,0:T(8,128)(2,1)}), bf16[32,1,256,768]{3,2,1,0:T(8,128)(2,1)}, u32[]{:S(2)}, u32[]{:S(2)}) async-start(bf16[32,1,256,768]{3,2,1,0:T(8,128)(2,1)} %stack.2), calls=%async_computation | async-start | bytes 25165824 | tf_op jit(solution)/shard_map/all_to_all | solution.py:79
  202.1 0.7 copy-start.10
  219.3 5.9 copy-start.12
  219.3 47.1 %all-to-all-start.2 = ((bf16[128,16,768]{2,1,0:T(8,128)(2,1)}), bf16[128,16,768]{2,1,0:T(8,128)(2,1)}, u32[]{:S(2)}, u32[]{:S(2)}) async-start(bf16[128,16,768]{2,1,0:T(8,128)(2,1)} %bitcast.67), calls=%async_computation.2 | async-start | bytes 6291456 | tf_op jit(solution)/shard_map/all_to_all | solution.py:96
  225.2 385.8 %reduce-scatter.11.cloned.1.call-start = ((), (), s32[]{:S(2)}) async-start(), calls=%async_computation.8 | async-start | bytes 3170304 | tf_op jit(solution)/shard_map/reduce_scatter | solution.py:115
  230.2 4.2 copy-start.14
  230.2 4.5 copy-start.22
  383.1 3.5 copy-start.2
  383.1 3.6 copy-start.3
  383.1 3.6 copy-start.4
  383.1 3.6 copy-start.5
  383.1 3.7 copy-start.6
  383.1 4.1 copy-start.7
  383.1 4.4 copy-start.8
  383.1 4.4 copy-start.16
  383.1 4.4 copy-start.17
  383.1 4.4 copy-start.18
  383.1 4.4 copy-start.19
  383.2 4.4 copy-start.20
  383.2 4.4 copy-start.21
  387.5 8.8 copy-start.9
  387.5 8.8 copy-start.13
  387.6 8.8 copy-start.26
  400.3 1.2 copy-start.27
  405.0 1.3 copy-start.11
  405.0 419.4 %reduce-scatter.9.cloned.1.call-start = ((), (), s32[]{:S(2)}) async-start(), calls=%async_computation.7 | async-start | bytes 3170304 | tf_op jit(solution)/shard_map/reduce_scatter | solution.py:114
  411.4 1064.3 %reduce-scatter.15.cloned.1.call-start = ((), (), s32[]{:S(2)}) async-start(), calls=%async_computation.10 | async-start | bytes 4227072
  427.1 1695.4 %reduce-scatter.13.cloned.1.call-start = ((), (), s32[]{:S(2)}) async-start(), calls=%async_computation.9 | async-start | bytes 4227072
  436.1 1.6 copy-start.1
Sparse Core Ops, SparseCore 0:
  405.1 205.8 reduce-scatter.10
  616.3 207.9 reduce-scatter.8
  827.3 648.3 reduce-scatter.14
  1478.4 644.0 reduce-scatter.12
